TPU v7x, 32 devices: a whole 2x2x4 slice. The times are simulated.
32 devices in a mesh: groups: 2 (over x), ctx: 16 (over z, y, core).
Axes of the slice: x: 2, y: 2, z: 4, core: 2. Of those that a mesh axis runs over, the one named last changes fastest.
Arguments:
- context_keys: bfloat16 [4096, 2048], P(('groups', 'ctx')), parts along dimension 0, may hold values from -6 to 6
- context_values: bfloat16 [4096, 2048], P(('groups', 'ctx')), parts along dimension 0, may hold values from -6 to 6
- context_queries: bfloat16 [4096, 2048], P(('groups', 'ctx')), parts along dimension 0, may hold values from -6 to 6
- token_rates: float32 [8, 4096], P(None, ('groups', 'ctx')), parts along dimension 1, may hold values from 0.05 to 1
- w_gate: bfloat16 [8, 256, 256], replicated, may hold values from -0.375 to 0.375
- w_up: bfloat16 [8, 256, 256], replicated, may hold values from -0.375 to 0.375
- w_down: bfloat16 [8, 256, 256], replicated, may hold values from -0.375 to 0.375
- question_rows: bfloat16 [8192, 2048], P(('groups', 'ctx')), parts along dimension 0, may hold values from -6 to 6
- question_count: int32 [32], P(('groups', 'ctx')), parts along dimension 0, may hold values from 1 to 256, 1024 in all
Outputs:
- context_out: bfloat16 [4096, 2048], P(('groups', 'ctx')), parts along dimension 0
- answers: bfloat16 [8192, 2048], P(('groups', 'ctx')), parts along dimension 0
There are 2 independent parts, one for each index of `groups`. A program takes and returns all parts, laid end to end along the dimension named above; an argument that names none is the same for every part. Nothing has to cross between parts.
Inputs may be any that keep to these rules, and one draw needn't show every extreme that they name: `question_count`: live rows are the first of each device's 256 slots. The counts of one user (the devices along ctx) add up to exactly 1024, and some device of each user has exactly 256.
All inputs are finite; a program needn't handle non-finite values.
Results may differ from a plain program's by a relative error of at most 0.018.
Values may be sent and summed in bfloat16 or wider, within the bound.
A program may use at most 128 MiB of HBM per device.

v0:
```python
import jax
import jax.numpy as jnp
from jax import lax
from jax.sharding import PartitionSpec as P

NS_STEPS = 3


quintic_first = 3.4445
quintic_second = -4.775
quintic_third = 2.0315


def fast_apply(in_rows, w_gate, w_up, w_down):
    head_count = w_gate.shape[0]
    head_size = w_gate.shape[1]
    row_split = in_rows.reshape(in_rows.shape[0], head_count, head_size)
    pre_gate = jnp.einsum("thd,hde->hte", row_split, w_gate, preferred_element_type=jnp.float32)
    pre_up = jnp.einsum("thd,hde->hte", row_split, w_up, preferred_element_type=jnp.float32)
    hidden = (jax.nn.silu(pre_gate) * pre_up).astype(jnp.bfloat16)
    outputs = jnp.einsum("hte,hef->thf", hidden, w_down, preferred_element_type=jnp.float32)
    return outputs.reshape(in_rows.shape[0], head_count * head_size).astype(jnp.bfloat16)


def directions(context_keys, context_values, token_rates, w_gate, w_up, w_down):
    tok_rows = context_keys.shape[0]
    head_count = w_gate.shape[0]
    head_size = w_gate.shape[1]
    key_split = context_keys.reshape(tok_rows, head_count, head_size)
    value_split = context_values.reshape(tok_rows, head_count, head_size)
    pre_gate = jnp.einsum("thd,hde->hte", key_split, w_gate, preferred_element_type=jnp.float32)
    pre_up = jnp.einsum("thd,hde->hte", key_split, w_up, preferred_element_type=jnp.float32)
    sigmoid_gate = jax.nn.sigmoid(pre_gate)
    activated = pre_gate * sigmoid_gate
    hidden = (activated * pre_up).astype(jnp.bfloat16)
    weighted = (token_rates.T[:, :, None] * value_split).astype(jnp.bfloat16)
    back_hidden = jnp.einsum("thf,hef->hte", weighted, w_down, preferred_element_type=jnp.float32)
    back_gate = (
        back_hidden * pre_up * sigmoid_gate * (1.0 + pre_gate * (1.0 - sigmoid_gate))
    ).astype(jnp.bfloat16)
    back_up = (back_hidden * activated).astype(jnp.bfloat16)
    step_gate = jnp.einsum("thd,hte->hde", key_split, back_gate, preferred_element_type=jnp.float32)
    step_up = jnp.einsum("thd,hte->hde", key_split, back_up, preferred_element_type=jnp.float32)
    step_down = jnp.einsum("hte,thf->hef", hidden, weighted, preferred_element_type=jnp.float32)
    return jnp.stack([step_gate, step_up, step_down])


def per_device(
    context_keys,
    context_values,
    context_queries,
    token_rates,
    w_gate,
    w_up,
    w_down,
    question_rows,
    question_count,
):
    head_count = w_gate.shape[0]
    head_size = w_gate.shape[1]
    matrix_count = 3 * head_count
    context_out = fast_apply(context_queries, w_gate, w_up, w_down)
    direction = directions(context_keys, context_values, token_rates, w_gate, w_up, w_down)
    flat_grads = direction.reshape(matrix_count, head_size * head_size)
    total = lax.psum(flat_grads, "ctx")
    norm_sizes = jnp.sqrt(jnp.sum(total * total, axis=1, keepdims=True))
    scaled = (total / (norm_sizes + 1e-06)).astype(jnp.bfloat16)
    iterate = scaled.reshape(matrix_count, head_size, head_size)
    for sweep_index in range(NS_STEPS):
        gram_matrix = jnp.einsum(
            "mij,mkj->mik", iterate, iterate, preferred_element_type=jnp.float32
        ).astype(jnp.bfloat16)
        gram_square = jnp.einsum(
            "mij,mjk->mik", gram_matrix, gram_matrix, preferred_element_type=jnp.float32
        )
        polynomial = (
            quintic_second * gram_matrix.astype(jnp.float32) + quintic_third * gram_square
        ).astype(jnp.bfloat16)
        product = jnp.einsum(
            "mij,mjk->mik", polynomial, iterate, preferred_element_type=jnp.float32
        )
        iterate = (quintic_first * iterate.astype(jnp.float32) + product).astype(jnp.bfloat16)
    previous = jnp.stack([w_gate, w_up, w_down]).astype(jnp.float32)
    moved = previous + iterate.reshape(3, head_count, head_size, head_size).astype(jnp.float32)
    col_norms = jnp.sqrt(jnp.sum(previous * previous, axis=2, keepdims=True))
    updated = (
        moved * col_norms / jnp.sqrt(jnp.sum(moved * moved, axis=2, keepdims=True) + 1e-06)
    ).astype(jnp.bfloat16)
    capacity = question_rows.shape[0]
    outputs = fast_apply(question_rows, updated[0], updated[1], updated[2])
    live_mask = jnp.arange(capacity, dtype=jnp.int32) < question_count[0]
    answers = jnp.where(live_mask[:, None], outputs, jnp.zeros_like(outputs))
    return (context_out, answers)


def solution(mesh):
    return jax.shard_map(
        per_device,
        mesh=mesh,
        in_specs=(
            P(("groups", "ctx"), None),
            P(("groups", "ctx"), None),
            P(("groups", "ctx"), None),
            P(None, ("groups", "ctx")),
            P(),
            P(),
            P(),
            P(("groups", "ctx"), None),
            P(("groups", "ctx")),
        ),
        out_specs=(P(("groups", "ctx"), None), P(("groups", "ctx"), None)),
        check_vma=False,
    )
```

profile of v0, /device:TPU:0, one launch (start us, length us, event | category | flops | bytes accessed | tf_op | source)
XLA Modules:
  0.0 236.1 jit_solution(8442899116746412055)
XLA Ops:
  7.3 1.8 fusion.41
  9.1 1.4 fusion.43
  11.1 0.7 convolution_bitcast_fusion
  12.1 0.6 convolution_bitcast_fusion.2
  13.4 3.3 %pad_maximum_fusion = f32[3,8,256,256]{2,3,1,0:T(8,128)} fusion(f32[1,8,256,256]{2,3,1,0:T(8,128)S(1)} %convolution_bitcast_fusion, f32[1,8,256,256]{2,3,1,0:T(8,128)S(1)} %convolution_bitcast_fusion.1, f32[1,8,256,256]{2,3,1,0:T(8,128)S(1)} %convolution_bitcast_fusion.2), kind=kLoop, calls=%fused_computation | loop fusion | flops 3145728 | bytes 12582912 | tf_op jit(solution)/shard_map/stack | solution.py:45
  16.7 6.7 %copy.60 = f32[3,8,256,256]{3,1,2,0:T(8,128)} copy(f32[3,8,256,256]{2,3,1,0:T(8,128)} %pad_maximum_fusion) | data formatting | bytes 12582912
  23.4 1.2 copy-done.7
  25.7 1.9 copy.33
  27.5 3.1 %maximum_convert_fusion = f32[3,8,256,256]{2,3,1,0:T(8,128)} fusion(bf16[1,8,256,256]{2,3,1,0:T(8,128)(2,1)S(1)} %bitcast.124, bf16[1,8,256,256]{2,3,1,0:T(8,128)(2,1)S(1)} %bitcast.121, bf16[1,8,256,256]{2,3,1,0:T(8,128)(2,1)S(1)} %bitcast.118), kind=kLoop, calls=%fused_computation.18 | loop fusion | flops 4718592 | bytes 9437184 | tf_op jit(solution)/shard_map/convert_element_type | solution.py:83
  30.6 7.0 %copy.45 = f32[3,8,256,256]{3,2,1,0:T(8,128)} copy(f32[3,8,256,256]{2,3,1,0:T(8,128)} %maximum_convert_fusion) | data formatting | bytes 12582912 | tf_op jit(solution)/shard_map/convert_element_type | solution.py:83
  37.6 1.0 multiply_reduce_fusion
  38.6 2.4 %copy.56 = bf16[256,2048]{0,1:T(8,128)(2,1)} copy(bf16[256,2048]{1,0:T(8,128)(2,1)} %param.16) | data formatting | bytes 2097152 | tf_op jit(solution)/shard_map/reshape | solution.py:17
  41.7 1.7 fusion.47
  43.4 2.5 %fusion.29 = bf16[128,8,256]{2,0,1:T(8,128)(2,1)} fusion(bf16[8,256,256]{2,1,0:T(8,128)(2,1)S(1)} %copy-done.10, bf16[8,256,256]{2,1,0:T(8,128)(2,1)S(1)} %copy-done.12, f32[8,128,256]{2,1,0:T(8,128)S(1)} %fusion.47, bf16[16,8,8,256]{3,2,1,0:T(8,128)(2,1)} %bitcast.140), kind=kOutput, calls=%fused_computation.45 | convolution fusion | flops 270270464 | bytes 4194304 | tf_op jit(solution)/shard_map/hte,hef->thf/dot_general | solution.py:21
  45.9 1.3 copy.30
  47.2 1.0 copy.49
  48.3 117.3 %all-reduce.2.cloned.1.call-done = f32[24,65536]{1,0:T(8,128)} async-done(((f32[24,65536]{1,0:T(8,128)}), f32[24,65536]{1,0:T(8,128)}) %all-reduce.2.cloned.1.call-update) | async-done | bytes 6291472 | tf_op jit(solution)/shard_map/psum | solution.py:65
  165.5 3.6 %multiply_reduce_fusion.1 = f32[24]{0:T(128)S(1)} fusion(f32[24,65536]{1,0:T(8,128)} %all-reduce.2.cloned.1.call-done), kind=kLoop, calls=%fused_computation.13 | loop fusion | flops 3145704 | bytes 6291552 | tf_op jit(solution)/shard_map/reduce_sum | solution.py:66
  169.1 1.0 copy-done
  170.5 0.7 copy.61
  171.3 2.7 %fusion.74 = bf16[24,256,256]{2,1,0:T(8,128)(2,1)} fusion(bf16[24,256,256]{2,1,0:T(8,128)(2,1)S(1)} %bitcast.115), kind=kOutput, calls=%fused_computation.96 | convolution fusion | flops 805306368 | bytes 6291456 | tf_op jit(solution)/shard_map/mij,mkj->mik/dot_general | solution.py:70
  173.9 7.8 %add_convert_fusion.4 = bf16[24,256,256]{2,1,0:T(8,128)(2,1)} fusion(bf16[24,256,256]{2,1,0:T(8,128)(2,1)S(1)} %bitcast.116, bf16[24,256,256]{2,1,0:T(8,128)(2,1)} %fusion.74), kind=kOutput, calls=%fused_computation.10 | convolution fusion | flops 1624768512 | bytes 9437184 | tf_op jit(solution)/shard_map/mij,mjk->mik/dot_general | solution.py:79
  181.8 5.5 %fusion.75 = bf16[24,256,256]{2,1,0:T(8,128)(2,1)} fusion(bf16[24,256,256]{2,1,0:T(8,128)(2,1)} %add_convert_fusion.4), kind=kOutput, calls=%fused_computation.97 | convolution fusion | flops 805306368 | bytes 6291456 | tf_op jit(solution)/shard_map/mij,mkj->mik/dot_general | solution.py:70
  187.3 8.2 %add_convert_fusion.2 = bf16[24,256,256]{2,1,0:T(8,128)(2,1)S(1)} fusion(bf16[24,256,256]{2,1,0:T(8,128)(2,1)} %add_convert_fusion.4, bf16[24,256,256]{2,1,0:T(8,128)(2,1)} %fusion.75), kind=kOutput, calls=%fused_computation.8 | convolution fusion | flops 1624768512 | bytes 9437184 | tf_op jit(solution)/shard_map/mij,mjk->mik/dot_general | solution.py:79
  195.5 2.7 %fusion.76 = bf16[24,256,256]{2,1,0:T(8,128)(2,1)} fusion(bf16[24,256,256]{2,1,0:T(8,128)(2,1)S(1)} %add_convert_fusion.2), kind=kOutput, calls=%fused_computation.98 | convolution fusion | flops 805306368 | bytes 6291456 | tf_op jit(solution)/shard_map/mij,mkj->mik/dot_general | solution.py:70
  198.1 11.6 %fusion.1 = (f32[24,256]{1,0:T(8,128)S(1)}, f32[24,256,256]{2,1,0:T(8,128)}) fusion(f32[3,8,256,256]{3,2,1,0:T(8,128)} %copy.45, bf16[24,256,256]{2,1,0:T(8,128)(2,1)S(1)} %add_convert_fusion.2, bf16[24,256,256]{2,1,0:T(8,128)(2,1)} %fusion.76), kind=kOutput, calls=%fused_computation.3 | convolution fusion | flops 1631053824 | bytes 18898944 | tf_op jit(solution)/shard_map/mij,mjk->mik/dot_general | solution.py:79
  209.7 6.7 %copy.44 = f32[3,8,256,256]{2,3,1,0:T(8,128)} copy(f32[3,8,256,256]{3,2,1,0:T(8,128)} %bitcast.128) | data formatting | bytes 12582912 | tf_op jit(solution)/shard_map/convert_element_type | solution.py:84
  216.5 4.6 %divide_convert_fusion = bf16[3,8,256,256]{2,3,1,0:T(8,128)(2,1)S(1)} fusion(f32[3,8,256,256]{2,3,1,0:T(8,128)} %copy.44, f32[3,8,256]{2,1,0:T(8,128)S(1)} %sqrt_bitcast_fusion, f32[3,8,256]{2,1,0:T(8,128)S(1)} %sqrt.28, bf16[1,8,256,256]{2,3,1,0:T(8,128)(2,1)S(1)} %bitcast.126, bf16[1,8,256,256]{2,3,1,0:T(8,128)(2,1)S(1)} %bitcast.123, ...), kind=kLoop, calls=%fused_computation.4 | loop fusion | flops 11010048 | bytes 12632064 | tf_op jit(solution)/shard_map/convert_element_type | solution.py:88
  221.1 1.6 copy-done.8
  223.1 3.5 %convolution_convert_fusion = bf16[8,256,256]{2,1,0:T(8,128)(2,1)} fusion(f32[8,256,256]{2,1,0:T(8,128)S(1)} %fusion.31, bf16[256,8,256]{0,2,1:T(8,128)(2,1)S(1)} %bitcast.132, bf16[3,8,256,256]{2,3,1,0:T(8,128)(2,1)} %copy-done.8), kind=kOutput, calls=%fused_computation.41 | convolution fusion | flops 540540928 | bytes 6291456 | tf_op jit(solution)/shard_map/hte,hef->thf/dot_general | solution.py:21
  226.7 1.5 copy.48
  228.2 1.1 broadcast_select_fusion
  (46 shorter events, 3.6 us)
Async XLA Ops:
  7.2 1.9 copy-start.11
  7.2 3.3 %copy-start.16 = (bf16[128,2048]{1,0:T(8,128)(2,1)S(1)}, bf16[128,2048]{1,0:T(8,128)(2,1)}, u32[]{:S(2)}) copy-start(bf16[128,2048]{1,0:T(8,128)(2,1)} %param.10) | copy-start | bytes 1572868
  7.2 158.3 %all-reduce.2.cloned.1.call-start = ((), (), s32[]{:S(2)}) async-start(), calls=%async_computation | async-start | bytes 12582912 | tf_op jit(solution)/shard_map/psum | solution.py:65
  7.2 3.4 %copy-start.9 = (bf16[8,256,256]{2,1,0:T(8,128)(2,1)S(1)}, bf16[8,256,256]{2,1,0:T(8,128)(2,1)}, u32[]{:S(2)}) copy-start(bf16[8,256,256]{2,1,0:T(8,128)(2,1)} %param.15) | copy-start | bytes 3145732
  7.2 3.3 %copy-start.17 = (f32[8,128]{1,0:T(8,128)S(1)}, f32[8,128]{1,0:T(8,128)}, u32[]{:S(2)}) copy-start(f32[8,128]{1,0:T(8,128)} %param.12) | copy-start | bytes 12292
  11.1 1.0 copy-start.15
  23.4 1.2 copy-start.7
  25.1 12.5 %copy-start.1 = (bf16[8,256,256]{1,2,0:T(8,128)(2,1)}, bf16[8,256,256]{1,2,0:T(8,128)(2,1)S(1)}, u32[]{:S(2)}) copy-start(bf16[8,256,256]{1,2,0:T(8,128)(2,1)S(1)} %copy.31) | copy-start | bytes 3145732
  25.6 11.9 %copy-start.3 = (bf16[8,256,256]{1,2,0:T(8,128)(2,1)}, bf16[8,256,256]{1,2,0:T(8,128)(2,1)S(1)}, u32[]{:S(2)}) copy-start(bf16[8,256,256]{1,2,0:T(8,128)(2,1)S(1)} %copy.32) | copy-start | bytes 3145732
  27.5 10.1 %copy-start.5 = (bf16[8,256,256]{1,2,0:T(8,128)(2,1)}, bf16[8,256,256]{1,2,0:T(8,128)(2,1)S(1)}, u32[]{:S(2)}) copy-start(bf16[8,256,256]{1,2,0:T(8,128)(2,1)S(1)} %copy.33) | copy-start | bytes 3145732
  38.6 4.8 %copy-start.10 = (bf16[8,256,256]{2,1,0:T(8,128)(2,1)S(1)}, bf16[8,256,256]{2,1,0:T(8,128)(2,1)}, u32[]{:S(2)}) copy-start(bf16[8,256,256]{2,1,0:T(8,128)(2,1)} %param.15) | copy-start | bytes 3145732
  38.6 4.8 %copy-start.12 = (bf16[8,256,256]{2,1,0:T(8,128)(2,1)S(1)}, bf16[8,256,256]{2,1,0:T(8,128)(2,1)}, u32[]{:S(2)}) copy-start(bf16[8,256,256]{2,1,0:T(8,128)(2,1)} %param.14) | copy-start | bytes 3145732
  165.5 4.6 %copy-start = (f32[24,65536]{1,0:T(8,128)S(1)}, f32[24,65536]{1,0:T(8,128)}, u32[]{:S(2)}) copy-start(f32[24,65536]{1,0:T(8,128)} %all-reduce.2.cloned.1.call-done) | copy-start | bytes 18874372
  209.7 6.7 %copy-start.2 = (bf16[8,256,256]{1,2,0:T(8,128)(2,1)S(1)}, bf16[8,256,256]{1,2,0:T(8,128)(2,1)}, u32[]{:S(2)}) copy-start(bf16[8,256,256]{1,2,0:T(8,128)(2,1)} %copy-done.1) | copy-start | bytes 3145732
  209.7 6.7 %copy-start.4 = (bf16[8,256,256]{1,2,0:T(8,128)(2,1)S(1)}, bf16[8,256,256]{1,2,0:T(8,128)(2,1)}, u32[]{:S(2)}) copy-start(bf16[8,256,256]{1,2,0:T(8,128)(2,1)} %copy-done.3) | copy-start | bytes 3145732
  209.7 6.7 %copy-start.6 = (bf16[8,256,256]{1,2,0:T(8,128)(2,1)S(1)}, bf16[8,256,256]{1,2,0:T(8,128)(2,1)}, u32[]{:S(2)}) copy-start(bf16[8,256,256]{1,2,0:T(8,128)(2,1)} %copy-done.5) | copy-start | bytes 3145732
  216.5 6.2 %copy-start.13 = (bf16[256,2048]{0,1:T(8,128)(2,1)S(1)}, bf16[256,2048]{0,1:T(8,128)(2,1)}, u32[]{:S(2)}) copy-start(bf16[256,2048]{0,1:T(8,128)(2,1)} %copy.56) | copy-start | bytes 3145732
  221.1 1.6 copy-start.8
  221.1 2.1 copy-start.14
Sparse Core Ops, SparseCore 0:
  23.5 141.9 all-reduce.1
where the time goes:
time: 237 us; the launch traced here: 236 us
  waiting for transfers between devices  117 us (49%)
  matrix products  52.2 us (22%)
  local copies, waits for them, and re-layouts  34.4 us (15%)
  other arithmetic  17.2 us (7%)
  between operations  15 us (6%)
    psum x1, waiting for transfers between devices, per_device(): total = lax.psum(flat_grads, 'ctx')  117 us
    dot_general x3, matrix products, per_device(): jnp.einsum('mij,mjk->mik', polynomial, iterate, preferred_element_type=jn...  27.6 us
    unnamed x42, local copies, waits for them, and re-layouts  15.6 us
    dot_general x3, matrix products, per_device(): jnp.einsum('mij,mkj->mik', iterate, iterate, preferred_element_type=jnp.f...  10.9 us
    convert_element_type x1, local copies, waits for them, and re-layouts, per_device(): previous = jnp.stack([w_gate, w_up, w_down]).astype(jnp.float32)  6.96 us
    convert_element_type x1, local copies, waits for them, and re-layouts, per_device(): iterate.reshape(3, head_count, head_size, head_size).astype(jnp.float32)  6.7 us
    dot_general x2, matrix products, fast_apply(): jnp.einsum('hte,hef->thf', hidden, w_down, preferred_element_type=jnp.flo...  6.01 us
  transfers between devices with their start and end apart: 1, of which 1 were waited for; matrix products, arithmetic and copies ran while one was open for 10% of the time, Pallas kernels for 0%

commit v1 on v0

--- a/solution.py
+++ b/solution.py
@@ -1,6 +1,10 @@
+import functools
+
 import jax
 import jax.numpy as jnp
 from jax import lax
+from jax.experimental import pallas as pl
+from jax.experimental.pallas import tpu as pltpu
 from jax.sharding import PartitionSpec as P
 
 NS_STEPS = 3
@@ -93,9 +97,329 @@
     return (context_out, answers)
 
 
+MESH = pl.DeviceIdType.MESH
+ROWS = 2
+
+
+def dot(a, b, contract=((1,), (0,))):
+    return lax.dot_general(a, b, (contract, ((), ())), preferred_element_type=jnp.float32)
+
+
+def read_memory(rows, gate, up, down):
+    pre_gate = dot(rows, gate)
+    pre_up = dot(rows, up)
+    hidden = (pre_gate * jax.nn.sigmoid(pre_gate) * pre_up).astype(jnp.bfloat16)
+    return dot(hidden, down).astype(jnp.bfloat16)
+
+
+def memory_kernel(
+    lines,
+    keys_hbm, values_ref, queries_hbm, rates_ref, gate_hbm, up_hbm, down_hbm, questions_hbm,
+    context_ref, answers_ref,
+    key_in, weighted_in, weighted_out, queries, gate, up, down, questions, acc, other_acc, gathered,
+    local_sem, key_send, key_recv, val_send, val_recv, acc_send, acc_recv,
+    up_send, down_send, cross_send, pair_send, line_recv, pair_recv,
+):
+    heads, size, _ = gate.shape
+    me = lax.axis_index("ctx")
+    core, chip = me % ROWS, me // ROWS
+    y, z = chip % ROWS, chip // ROWS
+    half = ROWS * size * 3 // 4
+
+    def device(a_chip, a_core):
+        return {"ctx": a_chip * ROWS + a_core}
+
+    def place(j):
+        return (z // 2 + j // 2) % (lines // 2) * 2 + (z + j) % 2
+
+    def columns(head):
+        return pl.ds(pl.multiple_of(head * size, size), size)
+
+    barrier = pltpu.get_barrier_semaphore()
+    for j in range(lines):
+        for dy in range(ROWS):
+            if j or dy:
+                peer = place(j) * ROWS + (y + dy) % ROWS
+                pl.semaphore_signal(barrier, inc=1, device_id=device(peer, core), device_id_type=MESH)
+    pl.semaphore_signal(barrier, inc=1, device_id=device(chip, 1 - core), device_id_type=MESH)
+
+    loads = [
+        pltpu.make_async_copy(src, dst, local_sem.at[i])
+        for i, (src, dst) in enumerate([
+            (gate_hbm, gate), (up_hbm, up), (down_hbm, down),
+            (queries_hbm, queries), (questions_hbm, questions),
+            (keys_hbm.at[:, columns(chip)], key_in.at[chip]),
+        ])
+    ]
+    for load in loads:
+        load.start()
+
+    rates = rates_ref[...].T
+    for head in range(heads):
+        cols = slice(head * size, (head + 1) * size)
+        weighted_out[head] = (
+            rates[:, head:head + 1] * values_ref[:, cols].astype(jnp.float32)
+        ).astype(jnp.bfloat16)
+    own_weighted = pltpu.make_async_copy(weighted_out.at[chip], weighted_in.at[chip], local_sem.at[6])
+
+    pl.semaphore_wait(barrier, lines * ROWS)
+    own_weighted.start()
+
+    def key_copy(to, slot):
+        return pltpu.make_async_remote_copy(
+            src_ref=keys_hbm.at[:, columns(to)], dst_ref=key_in.at[slot],
+            send_sem=key_send.at[to], recv_sem=key_recv.at[slot],
+            device_id=device(to, core), device_id_type=MESH)
+
+    def val_copy(to, slot):
+        return pltpu.make_async_remote_copy(
+            src_ref=weighted_out.at[to], dst_ref=weighted_in.at[slot],
+            send_sem=val_send.at[to], recv_sem=val_recv.at[slot],
+            device_id=device(to, core), device_id_type=MESH)
+
+    for j in reversed(range(lines)):
+        for dy in range(ROWS):
+            if j or dy:
+                to = place(j) * ROWS + (y + dy) % ROWS
+                key_copy(to, chip).start()
+                val_copy(to, chip).start()
+
+    for load in loads[:4]:
+        load.wait()
+
+    @pl.loop(0, heads)
+    def _(head):
+        context_ref[:, columns(head)] = read_memory(
+            queries[:, columns(head)], gate[head], up[head], down[head])
+
+    loads[5].wait()
+    own_weighted.wait()
+    acc[...] = jnp.zeros_like(acc)
+
+    @pl.loop(0, lines)
+    def _(j):
+        line = place(j)
+        for a_row in range(ROWS):
+            source = line * ROWS + a_row
+
+            @pl.when(source != chip)
+            def _():
+                key_copy(source, source).wait_recv()
+                val_copy(source, source).wait_recv()
+
+        pair = pl.ds(line * ROWS, ROWS)
+        key = key_in[pair].reshape(-1, size)
+        weighted = weighted_in[pair].reshape(-1, size)
+        pre_gate = dot(key, gate[chip])
+        pre_up = dot(key, up[chip])
+        back_hidden = dot(weighted, down[chip], ((1,), (1,)))
+        sigmoid = jax.nn.sigmoid(pre_gate)
+        active = pre_gate * sigmoid
+        hidden = (active * pre_up).astype(jnp.bfloat16)
+        back_gate = (
+            back_hidden * pre_up * sigmoid * (1.0 + pre_gate * (1.0 - sigmoid))
+        ).astype(jnp.bfloat16)
+        back_up = (back_hidden * active).astype(jnp.bfloat16)
+        acc[0] += dot(key, back_gate, ((0,), (0,)))
+        acc[1] += dot(key, back_up, ((0,), (0,)))
+        acc[2] += dot(hidden, weighted, ((0,), (0,)))
+
+    exchange = pltpu.make_async_remote_copy(
+        src_ref=acc, dst_ref=other_acc, send_sem=acc_send, recv_sem=acc_recv,
+        device_id=device(chip, 1 - core), device_id_type=MESH)
+    exchange.start()
+    exchange.wait()
+
+    matrices = []
+    for m in range(3):
+        total = acc[m] + other_acc[m]
+        norm = jnp.sqrt(jnp.sum(total * total, keepdims=True))
+        matrices.append((total / (norm + 1e-06)).astype(jnp.bfloat16))
+    for _ in range(NS_STEPS):
+        grams = [dot(x, x, ((1,), (1,))).astype(jnp.bfloat16) for x in matrices]
+        polys = [
+            (quintic_second * g.astype(jnp.float32) + quintic_third * dot(g, g)).astype(jnp.bfloat16)
+            for g in grams
+        ]
+        matrices = [
+            (quintic_first * x.astype(jnp.float32) + dot(p, x)).astype(jnp.bfloat16)
+            for p, x in zip(polys, matrices)
+        ]
+    for m, (initial, x) in enumerate(zip((gate, up, down), matrices)):
+        previous = initial[chip].astype(jnp.float32)
+        moved = previous + x.astype(jnp.float32)
+        norms = jnp.sqrt(jnp.sum(previous * previous, axis=0, keepdims=True))
+        gathered[chip, m * size:(m + 1) * size, :] = (
+            moved * norms / jnp.sqrt(jnp.sum(moved * moved, axis=0, keepdims=True) + 1e-06)
+        ).astype(jnp.bfloat16)
+
+    def hop(origin, part, send, recv, to_chip, to_core):
+        block = gathered.at[origin, pl.ds(pl.multiple_of(part * half, half), half)]
+        return pltpu.make_async_remote_copy(
+            src_ref=block, dst_ref=block, send_sem=send.at[origin], recv_sem=recv.at[origin],
+            device_id=device(to_chip, to_core), device_id_type=MESH)
+
+    def hop_up(origin):
+        return hop(origin, core, up_send, line_recv, chip + ROWS, core)
+
+    def hop_down(origin):
+        return hop(origin, core, down_send, line_recv, chip - ROWS, core)
+
+    def hop_cross(origin):
+        return hop(origin, core, cross_send, line_recv, z * ROWS + 1 - y, core)
+
+    def hop_pair(origin):
+        return hop(origin, core, pair_send, pair_recv, chip, 1 - core)
+
+    def from_pair(origin):
+        return hop(origin, 1 - core, pair_send, pair_recv, chip, 1 - core)
+
+    def answer(origin):
+        answers_ref[:, columns(origin)] = read_memory(
+            questions[:, columns(origin)],
+            gathered[origin, 0:size, :],
+            gathered[origin, size:2 * size, :],
+            gathered[origin, 2 * size:3 * size, :])
+
+    @pl.when(z + 1 < lines)
+    def _():
+        hop_up(chip).start()
+
+    @pl.when(z > 0)
+    def _():
+        hop_down(chip).start()
+
+    hop_cross(chip).start()
+    loads[4].wait()
+    answer(chip)
+
+    @pl.loop(1, lines + 2)
+    def _(k):
+        @pl.when(z - k >= 0)
+        def _():
+            origin = chip - ROWS * k
+            hop_cross(origin).wait_recv()
+
+            @pl.when(z + 1 < lines)
+            def _():
+                hop_up(origin).start()
+
+            hop_cross(origin).start()
+            hop_pair(origin).start()
+
+        @pl.when(z + k < lines)
+        def _():
+            origin = chip + ROWS * k
+            hop_cross(origin).wait_recv()
+
+            @pl.when(z > 0)
+            def _():
+                hop_down(origin).start()
+
+            hop_cross(origin).start()
+            hop_pair(origin).start()
+
+        def crossed(line):
+            origin = line * ROWS + 1 - y
+            hop_cross(origin).wait_recv()
+            hop_pair(origin).start()
+
+        def finish(origin):
+            from_pair(origin).wait_recv()
+            answer(origin)
+
+        near = k - 1
+        last = k - 2
+        pl.when(z - near >= 0)(lambda: crossed(z - near))
+        pl.when((near > 0) & (z + near < lines))(lambda: crossed(z + near))
+        pl.when((near > 0) & (z - near >= 0))(lambda: finish((z - near) * ROWS + y))
+        pl.when((near > 0) & (z + near < lines))(lambda: finish((z + near) * ROWS + y))
+        pl.when((last >= 0) & (z - last >= 0))(lambda: finish((z - last) * ROWS + 1 - y))
+        pl.when((last > 0) & (z + last < lines))(lambda: finish((z + last) * ROWS + 1 - y))
+
+    @pl.loop(0, lines)
+    def _(line):
+        mine = line * ROWS + y
+        across = line * ROWS + 1 - y
+        pl.when((line <= z) & (z + 1 < lines))(lambda: hop_up(mine).wait_send())
+        pl.when((line >= z) & (z > 0))(lambda: hop_down(mine).wait_send())
+        hop_cross(mine).wait_send()
+        hop_pair(across).wait_send()
+        key_copy(across, across).wait_send()
+        val_copy(across, across).wait_send()
+
+        @pl.when(line != z)
+        def _():
+            hop_pair(mine).wait_send()
+            key_copy(mine, mine).wait_send()
+            val_copy(mine, mine).wait_send()
+
+
+def head_per_chip(
+    lines,
+    context_keys,
+    context_values,
+    context_queries,
+    token_rates,
+    w_gate,
+    w_up,
+    w_down,
+    question_rows,
+    question_count,
+):
+    heads, size, _ = w_gate.shape
+    tokens, width = context_keys.shape
+    capacity = question_rows.shape[0]
+    vmem = pl.BlockSpec(memory_space=pltpu.VMEM)
+    anywhere = pl.BlockSpec(memory_space=pl.ANY)
+    sem = pltpu.SemaphoreType.DMA
+    half_type = jnp.bfloat16
+    context_out, outputs = pl.pallas_call(
+        functools.partial(memory_kernel, lines),
+        out_shape=(
+            jax.ShapeDtypeStruct((tokens, width), half_type),
+            jax.ShapeDtypeStruct((capacity, width), half_type),
+        ),
+        in_specs=[anywhere, vmem, anywhere, vmem, anywhere, anywhere, anywhere, anywhere],
+        out_specs=(vmem, vmem),
+        scratch_shapes=[
+            pltpu.VMEM((heads, tokens, size), half_type),
+            pltpu.VMEM((heads, tokens, size), half_type),
+            pltpu.VMEM((heads, tokens, size), half_type),
+            pltpu.VMEM((tokens, width), half_type),
+            pltpu.VMEM((heads, size, size), half_type),
+            pltpu.VMEM((heads, size, size), half_type),
+            pltpu.VMEM((heads, size, size), half_type),
+            pltpu.VMEM((capacity, width), half_type),
+            pltpu.VMEM((3, size, size), jnp.float32),
+            pltpu.VMEM((3, size, size), jnp.float32),
+            pltpu.VMEM((heads, 3 * size, size), half_type),
+            sem((7,)),
+            sem((heads,)), sem((heads,)), sem((heads,)), sem((heads,)),
+            sem, sem,
+            sem((heads,)), sem((heads,)), sem((heads,)), sem((heads,)),
+            sem((heads,)), sem((heads,)),
+        ],
+        compiler_params=pltpu.CompilerParams(
+            collective_id=0, has_side_effects=True, vmem_limit_bytes=48 * 1024 * 1024
+        ),
+    )(context_keys, context_values, context_queries, token_rates, w_gate, w_up, w_down, question_rows)
+    live_mask = jnp.arange(capacity, dtype=jnp.int32) < question_count[0]
+    return context_out, jnp.where(live_mask[:, None], outputs, jnp.zeros_like(outputs))
+
+
 def solution(mesh):
+    members = mesh.shape["ctx"]
+    lines = members // (ROWS * ROWS)
+
+    def body(*arrays):
+        heads = arrays[4].shape[0]
+        if members == ROWS * heads and lines % 2 == 0:
+            return head_per_chip(lines, *arrays)
+        return per_device(*arrays)
+
     return jax.shard_map(
-        per_device,
+        body,
         mesh=mesh,
         in_specs=(
             P(("groups", "ctx"), None),

time: 237 us -> 69.5 us (0.29)
  waiting for transfers between devices: 117 us -> 0 us
  Pallas kernels: 0 us -> 60.3 us
  matrix products: 52.2 us -> 0 us
  local copies, waits for them, and re-layouts: 34.4 us -> 6.37 us
  other arithmetic: 17.2 us -> 1.12 us
  between operations: 15 us -> 1.33 us
    psum x1 -> x0, waiting for transfers between devices: 117 us -> none  [per_device(): total = lax.psum(flat_grads, 'ctx')]
    pallas_call x0 -> x1, Pallas kernels: none -> 60.3 us  [head_per_chip(): pl.pallas_call(functools.partial(memory_kernel, lines), out_shape=(jax.Sh...]
    dot_general x16 -> x0, matrix products: 52.2 us -> none  [the longest x3 27.6 us: per_device(): jnp.einsum('mij,mjk->mik', polynomial, iterate, preferred_element_type=jn...]
    convert_element_type x4 -> x0, local copies, waits for them, and re-layouts: 16.5 us -> none  [the longest x1 6.96 us: per_device(): previous = jnp.stack([w_gate, w_up, w_down]).astype(jnp.float32)]
    unnamed x42 -> x13, local copies, waits for them, and re-layouts: 15.6 us -> 6.37 us
    convert_element_type x4 -> x0, other arithmetic: 8.14 us -> none  [the longest x1 4.55 us: per_device(): updated = (moved * col_norms / jnp.sqrt(jnp.sum(moved * moved, axis=2, ke...]
    reduce_sum x2 -> x0, other arithmetic: 4.58 us -> none  [the longest x1 3.58 us: per_device(): norm_sizes = jnp.sqrt(jnp.sum(total * total, axis=1, keepdims=True))]
    another operation x1 -> x0, other arithmetic: 3.31 us -> none  [directions(): return jnp.stack([step_gate, step_up, step_down])]
  transfers between devices with their start and end apart: 1 -> 0, of which waited for: 1 -> 0; matrix products, arithmetic and copies ran while one was open for 10% -> 0% of each run, Pallas kernels for 0% -> 0%
where the time goes in v1:
time: 69.5 us; the launch traced here: 69.1 us
  Pallas kernels  60.3 us (87%)
  local copies, waits for them, and re-layouts  6.37 us (9%)
  between operations  1.33 us (2%)
  other arithmetic  1.12 us (2%)
    pallas_call x1, Pallas kernels, head_per_chip(): pl.pallas_call(functools.partial(memory_kernel, lines), out_shape=(jax.Sh...  60.3 us
    unnamed x13, local copies, waits for them, and re-layouts  6.37 us

profile of v1, /device:TPU:0, one launch (start us, length us, event | category | flops | bytes accessed | tf_op | source)
XLA Modules:
  0.0 69.1 jit_solution(14743800724722369213)
XLA Ops:
  0.6 0.0 copy-start.5
  1.3 0.0 copy-done.5
  1.3 0.0 copy-start
  1.3 1.2 %copy-done = bf16[8,256,256]{2,1,0:T(8,128)(2,1)S(1)} copy-done((bf16[8,256,256]{2,1,0:T(8,128)(2,1)S(1)}, bf16[8,256,256]{2,1,0:T(8,128)(2,1)}, u32[]{:S(2)}) %copy-start) | copy-done | bytes 1048600
  2.5 0.0 copy-start.1
  2.6 1.2 %copy-done.1 = bf16[8,256,256]{2,1,0:T(8,128)(2,1)S(1)} copy-done((bf16[8,256,256]{2,1,0:T(8,128)(2,1)S(1)}, bf16[8,256,256]{2,1,0:T(8,128)(2,1)}, u32[]{:S(2)}) %copy-start.1) | copy-done | bytes 1048600
  3.8 0.0 copy-start.2
  3.8 1.0 %copy-done.2 = bf16[128,2048]{1,0:T(8,128)(2,1)S(1)} copy-done((bf16[128,2048]{1,0:T(8,128)(2,1)S(1)}, bf16[128,2048]{1,0:T(8,128)(2,1)}, u32[]{:S(2)}) %copy-start.2) | copy-done | bytes 524312
  4.8 0.0 copy-start.3
  4.8 1.0 %copy-done.3 = bf16[128,2048]{1,0:T(8,128)(2,1)S(1)} copy-done((bf16[128,2048]{1,0:T(8,128)(2,1)S(1)}, bf16[128,2048]{1,0:T(8,128)(2,1)}, u32[]{:S(2)}) %copy-start.3) | copy-done | bytes 524312
  5.9 0.0 copy-start.4
  5.9 1.0 %copy-done.4 = bf16[128,2048]{1,0:T(8,128)(2,1)S(1)} copy-done((bf16[128,2048]{1,0:T(8,128)(2,1)S(1)}, bf16[128,2048]{1,0:T(8,128)(2,1)}, u32[]{:S(2)}) %copy-start.4) | copy-done | bytes 524312
  6.9 60.3 %shard_map.104 = (bf16[128,2048]{1,0:T(8,128)(2,1)S(1)}, bf16[256,2048]{1,0:T(8,128)(2,1)S(1)}) custom-call(bf16[128,2048]{1,0:T(8,128)(2,1)S(1)} %copy-done.2, bf16[128,2048]{1,0:T(8,128)(2,1)S(1)} %copy-done.3, bf16[128,2048]{1,0:T(8,128)(2,1)S(1)} %copy-done.4, f32[8,128]{1,0:T(8,128)S(1)} %copy-done.5, bf16[8,256,256]{2,1,0:T(8,128)(2,1)S(1)} %copy-done, ...), custom_call_target="tpu_custom_call" | custom-call | tf_op jit(solution)/shard_map/pallas_call | solution.py:377
  67.2 1.1 %broadcast_select_fusion = bf16[256,2048]{1,0:T(8,128)(2,1)} fusion(bf16[256,2048]{1,0:T(8,128)(2,1)S(1)} %get-tuple-element.5, pred[256]{0:T(512)(128)(4,1)S(1)} %iota_compare_fusion), kind=kLoop, calls=%fused_computation | loop fusion | flops 524288 | bytes 2097408 | tf_op jit(solution)/shard_map/jit(_where)/select_n | solution.py:408
  68.3 0.8 %copy.13 = bf16[128,2048]{1,0:T(8,128)(2,1)} copy(bf16[128,2048]{1,0:T(8,128)(2,1)S(1)} %get-tuple-element.8) | data formatting | bytes 1048576
  (1 shorter events, 0.0 us)
Async XLA Ops:
  0.6 0.7 copy-start.5
  1.3 1.2 %copy-start = (bf16[8,256,256]{2,1,0:T(8,128)(2,1)S(1)}, bf16[8,256,256]{2,1,0:T(8,128)(2,1)}, u32[]{:S(2)}) copy-start(bf16[8,256,256]{2,1,0:T(8,128)(2,1)} %gate_hbm.1) | copy-start | bytes 3145732
  2.5 1.2 %copy-start.1 = (bf16[8,256,256]{2,1,0:T(8,128)(2,1)S(1)}, bf16[8,256,256]{2,1,0:T(8,128)(2,1)}, u32[]{:S(2)}) copy-start(bf16[8,256,256]{2,1,0:T(8,128)(2,1)} %up_hbm.1) | copy-start | bytes 3145732
  3.8 1.0 %copy-start.2 = (bf16[128,2048]{1,0:T(8,128)(2,1)S(1)}, bf16[128,2048]{1,0:T(8,128)(2,1)}, u32[]{:S(2)}) copy-start(bf16[128,2048]{1,0:T(8,128)(2,1)} %keys_hbm.1) | copy-start | bytes 1572868
  4.8 1.0 %copy-start.3 = (bf16[128,2048]{1,0:T(8,128)(2,1)S(1)}, bf16[128,2048]{1,0:T(8,128)(2,1)}, u32[]{:S(2)}) copy-start(bf16[128,2048]{1,0:T(8,128)(2,1)} %values_ref.1) | copy-start | bytes 1572868
  5.9 1.0 %copy-start.4 = (bf16[128,2048]{1,0:T(8,128)(2,1)S(1)}, bf16[128,2048]{1,0:T(8,128)(2,1)}, u32[]{:S(2)}) copy-start(bf16[128,2048]{1,0:T(8,128)(2,1)} %queries_hbm.1) | copy-start | bytes 1572868

commit v2 on v1

--- a/solution.py
+++ b/solution.py
@@ -98,6 +98,7 @@
 
 
 MESH = pl.DeviceIdType.MESH
+PIECES = 2
 ROWS = 2
 
 
@@ -114,9 +115,9 @@
 
 def memory_kernel(
     lines,
-    keys_hbm, values_ref, queries_hbm, rates_ref, gate_hbm, up_hbm, down_hbm, questions_hbm,
+    keys_hbm, values_hbm, queries_hbm, rates_hbm, gate_hbm, up_hbm, down_hbm, questions_hbm,
     context_ref, answers_ref,
-    key_in, weighted_in, weighted_out, queries, gate, up, down, questions, acc, other_acc, gathered,
+    key_in, weighted_in, weighted_out, values, rates_in, queries, gate, up, down, questions, acc, other_acc, gathered,
     local_sem, key_send, key_recv, val_send, val_recv, acc_send, acc_recv,
     up_send, down_send, cross_send, pair_send, line_recv, pair_recv,
 ):
@@ -124,7 +125,8 @@
     me = lax.axis_index("ctx")
     core, chip = me % ROWS, me // ROWS
     y, z = chip % ROWS, chip // ROWS
-    half = ROWS * size * 3 // 4
+    half = 3 * size // ROWS
+    piece = half // PIECES
 
     def device(a_chip, a_core):
         return {"ctx": a_chip * ROWS + a_core}
@@ -146,21 +148,24 @@
     loads = [
         pltpu.make_async_copy(src, dst, local_sem.at[i])
         for i, (src, dst) in enumerate([
-            (gate_hbm, gate), (up_hbm, up), (down_hbm, down),
-            (queries_hbm, queries), (questions_hbm, questions),
+            (rates_hbm, rates_in), (values_hbm, values),
             (keys_hbm.at[:, columns(chip)], key_in.at[chip]),
+            (queries_hbm, queries), (gate_hbm, gate), (up_hbm, up), (down_hbm, down),
+            (questions_hbm, questions),
         ])
     ]
     for load in loads:
         load.start()
 
-    rates = rates_ref[...].T
+    loads[0].wait()
+    loads[1].wait()
+    rates = rates_in[...].T
     for head in range(heads):
         cols = slice(head * size, (head + 1) * size)
         weighted_out[head] = (
-            rates[:, head:head + 1] * values_ref[:, cols].astype(jnp.float32)
+            rates[:, head:head + 1] * values[:, cols].astype(jnp.float32)
         ).astype(jnp.bfloat16)
-    own_weighted = pltpu.make_async_copy(weighted_out.at[chip], weighted_in.at[chip], local_sem.at[6])
+    own_weighted = pltpu.make_async_copy(weighted_out.at[chip], weighted_in.at[chip], local_sem.at[8])
 
     pl.semaphore_wait(barrier, lines * ROWS)
     own_weighted.start()
@@ -184,7 +189,7 @@
                 key_copy(to, chip).start()
                 val_copy(to, chip).start()
 
-    for load in loads[:4]:
+    for load in loads[2:7]:
         load.wait()
 
     @pl.loop(0, heads)
@@ -192,7 +197,6 @@
         context_ref[:, columns(head)] = read_memory(
             queries[:, columns(head)], gate[head], up[head], down[head])
 
-    loads[5].wait()
     own_weighted.wait()
     acc[...] = jnp.zeros_like(acc)
 
@@ -253,26 +257,28 @@
             moved * norms / jnp.sqrt(jnp.sum(moved * moved, axis=0, keepdims=True) + 1e-06)
         ).astype(jnp.bfloat16)
 
-    def hop(origin, part, send, recv, to_chip, to_core):
-        block = gathered.at[origin, pl.ds(pl.multiple_of(part * half, half), half)]
+    def hop(origin, p, part, send, recv, to_chip, to_core):
+        rows = pl.ds(pl.multiple_of(part * half + p * piece, piece), piece)
+        block = gathered.at[origin, rows]
+        slot = origin * PIECES + p
         return pltpu.make_async_remote_copy(
-            src_ref=block, dst_ref=block, send_sem=send.at[origin], recv_sem=recv.at[origin],
+            src_ref=block, dst_ref=block, send_sem=send.at[slot], recv_sem=recv.at[slot],
             device_id=device(to_chip, to_core), device_id_type=MESH)
 
-    def hop_up(origin):
-        return hop(origin, core, up_send, line_recv, chip + ROWS, core)
-
-    def hop_down(origin):
-        return hop(origin, core, down_send, line_recv, chip - ROWS, core)
-
-    def hop_cross(origin):
-        return hop(origin, core, cross_send, line_recv, z * ROWS + 1 - y, core)
-
-    def hop_pair(origin):
-        return hop(origin, core, pair_send, pair_recv, chip, 1 - core)
-
-    def from_pair(origin):
-        return hop(origin, 1 - core, pair_send, pair_recv, chip, 1 - core)
+    def hop_up(origin, p):
+        return hop(origin, p, core, up_send, line_recv, chip + ROWS, core)
+
+    def hop_down(origin, p):
+        return hop(origin, p, core, down_send, line_recv, chip - ROWS, core)
+
+    def hop_cross(origin, p):
+        return hop(origin, p, core, cross_send, line_recv, z * ROWS + 1 - y, core)
+
+    def hop_pair(origin, p):
+        return hop(origin, p, core, pair_send, pair_recv, chip, 1 - core)
+
+    def from_pair(origin, p):
+        return hop(origin, p, 1 - core, pair_send, pair_recv, chip, 1 - core)
 
     def answer(origin):
         answers_ref[:, columns(origin)] = read_memory(
@@ -281,78 +287,96 @@
             gathered[origin, size:2 * size, :],
             gathered[origin, 2 * size:3 * size, :])
 
-    @pl.when(z + 1 < lines)
+    def early(line):
+        return (core == 0) & ((line == 0) | (line == lines - 1))
+
+    def late(line):
+        return jnp.logical_not(early(line))
+
+    has_up, has_down = z + 1 < lines, z > 0
+
+    def mine(line):
+        return line * ROWS + y
+
+    def across(line):
+        return line * ROWS + 1 - y
+
+    for p in range(PIECES):
+        hop_cross(chip, p).start()
+        pl.when(has_up)(lambda: hop_up(chip, p).start())
+        pl.when(has_down)(lambda: hop_down(chip, p).start())
+
+    @pl.when(early(z))
     def _():
-        hop_up(chip).start()
-
-    @pl.when(z > 0)
-    def _():
-        hop_down(chip).start()
-
-    hop_cross(chip).start()
-    loads[4].wait()
+        for p in range(PIECES):
+            hop_cross(across(z), p).wait_recv()
+            pl.when(has_up)(lambda: hop_up(across(z), p).start())
+            pl.when(has_down)(lambda: hop_down(across(z), p).start())
+            hop_pair(across(z), p).start()
+
+    loads[7].wait()
     answer(chip)
+
+    def along(line, has_next, next_hop):
+        for p in range(PIECES):
+            origin = mine(line)
+            hop_cross(origin, p).wait_recv()
+            pl.when(has_next)(lambda: next_hop(origin, p).start())
+            pl.when(late(line))(lambda: hop_cross(origin, p).start())
+            hop_pair(origin, p).start()
+
+        @pl.when(early(line))
+        def _():
+            for p in range(PIECES):
+                hop_cross(across(line), p).wait_recv()
+                pl.when(has_next)(lambda: next_hop(across(line), p).start())
+                hop_pair(across(line), p).start()
+
+    def crossed(line):
+        @pl.when(late(line))
+        def _():
+            for p in range(PIECES):
+                hop_cross(across(line), p).wait_recv()
+                hop_pair(across(line), p).start()
+
+    def finish(origin):
+        for p in range(PIECES):
+            from_pair(origin, p).wait_recv()
+        answer(origin)
 
     @pl.loop(1, lines + 2)
     def _(k):
-        @pl.when(z - k >= 0)
-        def _():
-            origin = chip - ROWS * k
-            hop_cross(origin).wait_recv()
-
-            @pl.when(z + 1 < lines)
-            def _():
-                hop_up(origin).start()
-
-            hop_cross(origin).start()
-            hop_pair(origin).start()
-
-        @pl.when(z + k < lines)
-        def _():
-            origin = chip + ROWS * k
-            hop_cross(origin).wait_recv()
-
-            @pl.when(z > 0)
-            def _():
-                hop_down(origin).start()
-
-            hop_cross(origin).start()
-            hop_pair(origin).start()
-
-        def crossed(line):
-            origin = line * ROWS + 1 - y
-            hop_cross(origin).wait_recv()
-            hop_pair(origin).start()
-
-        def finish(origin):
-            from_pair(origin).wait_recv()
-            answer(origin)
-
+        pl.when(z - k >= 0)(lambda: along(z - k, has_up, hop_up))
+        pl.when(z + k < lines)(lambda: along(z + k, has_down, hop_down))
         near = k - 1
         last = k - 2
         pl.when(z - near >= 0)(lambda: crossed(z - near))
         pl.when((near > 0) & (z + near < lines))(lambda: crossed(z + near))
-        pl.when((near > 0) & (z - near >= 0))(lambda: finish((z - near) * ROWS + y))
-        pl.when((near > 0) & (z + near < lines))(lambda: finish((z + near) * ROWS + y))
-        pl.when((last >= 0) & (z - last >= 0))(lambda: finish((z - last) * ROWS + 1 - y))
-        pl.when((last > 0) & (z + last < lines))(lambda: finish((z + last) * ROWS + 1 - y))
+        pl.when((near > 0) & (z - near >= 0))(lambda: finish(mine(z - near)))
+        pl.when((near > 0) & (z + near < lines))(lambda: finish(mine(z + near)))
+        pl.when((last >= 0) & (z - last >= 0))(lambda: finish(across(z - last)))
+        pl.when((last > 0) & (z + last < lines))(lambda: finish(across(z + last)))
 
     @pl.loop(0, lines)
     def _(line):
-        mine = line * ROWS + y
-        across = line * ROWS + 1 - y
-        pl.when((line <= z) & (z + 1 < lines))(lambda: hop_up(mine).wait_send())
-        pl.when((line >= z) & (z > 0))(lambda: hop_down(mine).wait_send())
-        hop_cross(mine).wait_send()
-        hop_pair(across).wait_send()
-        key_copy(across, across).wait_send()
-        val_copy(across, across).wait_send()
+        goes_up = (line <= z) & has_up
+        goes_down = (line >= z) & has_down
+        key_copy(across(line), across(line)).wait_send()
+        val_copy(across(line), across(line)).wait_send()
 
         @pl.when(line != z)
         def _():
-            hop_pair(mine).wait_send()
-            key_copy(mine, mine).wait_send()
-            val_copy(mine, mine).wait_send()
+            key_copy(mine(line), mine(line)).wait_send()
+            val_copy(mine(line), mine(line)).wait_send()
+
+        for p in range(PIECES):
+            pl.when(goes_up & early(line))(lambda: hop_up(across(line), p).wait_send())
+            pl.when(goes_down & early(line))(lambda: hop_down(across(line), p).wait_send())
+            pl.when(goes_up)(lambda: hop_up(mine(line), p).wait_send())
+            pl.when(goes_down)(lambda: hop_down(mine(line), p).wait_send())
+            pl.when(late(line) | (line == z))(lambda: hop_cross(mine(line), p).wait_send())
+            hop_pair(across(line), p).wait_send()
+            pl.when(line != z)(lambda: hop_pair(mine(line), p).wait_send())
 
 
 def head_per_chip(
@@ -371,7 +395,6 @@
     tokens, width = context_keys.shape
     capacity = question_rows.shape[0]
     vmem = pl.BlockSpec(memory_space=pltpu.VMEM)
-    anywhere = pl.BlockSpec(memory_space=pl.ANY)
     sem = pltpu.SemaphoreType.DMA
     half_type = jnp.bfloat16
     context_out, outputs = pl.pallas_call(
@@ -380,12 +403,14 @@
             jax.ShapeDtypeStruct((tokens, width), half_type),
             jax.ShapeDtypeStruct((capacity, width), half_type),
         ),
-        in_specs=[anywhere, vmem, anywhere, vmem, anywhere, anywhere, anywhere, anywhere],
+        in_specs=[pl.BlockSpec(memory_space=pltpu.HBM)] * 8,
         out_specs=(vmem, vmem),
         scratch_shapes=[
             pltpu.VMEM((heads, tokens, size), half_type),
             pltpu.VMEM((heads, tokens, size), half_type),
             pltpu.VMEM((heads, tokens, size), half_type),
+            pltpu.VMEM((tokens, width), half_type),
+            pltpu.VMEM((heads, tokens), jnp.float32),
             pltpu.VMEM((tokens, width), half_type),
             pltpu.VMEM((heads, size, size), half_type),
             pltpu.VMEM((heads, size, size), half_type),
@@ -394,16 +419,21 @@
             pltpu.VMEM((3, size, size), jnp.float32),
             pltpu.VMEM((3, size, size), jnp.float32),
             pltpu.VMEM((heads, 3 * size, size), half_type),
-            sem((7,)),
+            sem((9,)),
             sem((heads,)), sem((heads,)), sem((heads,)), sem((heads,)),
             sem, sem,
-            sem((heads,)), sem((heads,)), sem((heads,)), sem((heads,)),
-            sem((heads,)), sem((heads,)),
+            *[sem((heads * PIECES,))] * 6,
         ],
         compiler_params=pltpu.CompilerParams(
             collective_id=0, has_side_effects=True, vmem_limit_bytes=48 * 1024 * 1024
         ),
-    )(context_keys, context_values, context_queries, token_rates, w_gate, w_up, w_down, question_rows)
+    )(*(
+        pltpu.with_memory_space_constraint(array, pltpu.HBM)
+        for array in (
+            context_keys, context_values, context_queries, token_rates,
+            w_gate, w_up, w_down, question_rows,
+        )
+    ))
     live_mask = jnp.arange(capacity, dtype=jnp.int32) < question_count[0]
     return context_out, jnp.where(live_mask[:, None], outputs, jnp.zeros_like(outputs))
 

time: 69.5 us -> 62.2 us (0.89)
  local copies, waits for them, and re-layouts: 6.37 us -> 0.79 us
  Pallas kernels: 60.3 us -> 58.8 us
    unnamed x13 -> x1, local copies, waits for them, and re-layouts: 6.37 us -> 0.79 us
    pallas_call x1, Pallas kernels: 60.3 us -> 58.8 us  [head_per_chip(): pl.pallas_call(functools.partial(memory_kernel, lines), out_shape=(jax.Sh...]
where the time goes in v2:
time: 62.2 us; the launch traced here: 62 us
  Pallas kernels  58.8 us (95%)
  between operations  1.29 us (2%)
  other arithmetic  1.12 us (2%)
  local copies, waits for them, and re-layouts  0.79 us (1%)
    pallas_call x1, Pallas kernels, head_per_chip(): pl.pallas_call(functools.partial(memory_kernel, lines), out_shape=(jax.Sh...  58.8 us

profile of v2, /device:TPU:0, one launch (start us, length us, event | category | flops | bytes accessed | tf_op | source)
XLA Modules:
  0.0 62.0 jit_solution(2355344442781670180)
XLA Ops:
  1.3 58.8 %shard_map.104 = (bf16[128,2048]{1,0:T(8,128)(2,1)S(1)}, bf16[256,2048]{1,0:T(8,128)(2,1)S(1)}) custom-call(bf16[128,2048]{1,0:T(8,128)(2,1)} %keys_hbm.1, bf16[128,2048]{1,0:T(8,128)(2,1)} %values_hbm.1, bf16[128,2048]{1,0:T(8,128)(2,1)} %queries_hbm.1, f32[8,128]{1,0:T(8,128)} %rates_hbm.1, bf16[8,256,256]{2,1,0:T(8,128)(2,1)} %gate_hbm.1, ...), custom_call_target="tpu_custom_call" | custom-call | tf_op jit(solution)/shard_map/pallas_call | solution.py:400
  60.1 1.1 %broadcast_select_fusion = bf16[256,2048]{1,0:T(8,128)(2,1)} fusion(bf16[256,2048]{1,0:T(8,128)(2,1)S(1)} %get-tuple-element.5, pred[256]{0:T(512)(128)(4,1)S(1)} %iota_compare_fusion), kind=kLoop, calls=%fused_computation | loop fusion | flops 524288 | bytes 2097408 | tf_op jit(solution)/shard_map/jit(_where)/select_n | solution.py:438
  61.2 0.8 %copy.13 = bf16[128,2048]{1,0:T(8,128)(2,1)} copy(bf16[128,2048]{1,0:T(8,128)(2,1)S(1)} %get-tuple-element.8) | data formatting | bytes 1048576
  (1 shorter events, 0.0 us)

commit v3 on v2

--- a/solution.py
+++ b/solution.py
@@ -117,8 +117,8 @@
     lines,
     keys_hbm, values_hbm, queries_hbm, rates_hbm, gate_hbm, up_hbm, down_hbm, questions_hbm,
     context_ref, answers_ref,
-    key_in, weighted_in, weighted_out, values, rates_in, queries, gate, up, down, questions, acc, other_acc, gathered,
-    local_sem, key_send, key_recv, val_send, val_recv, acc_send, acc_recv,
+    key_in, weighted_in, weighted_out, values, rates_in, queries, gate, up, down, questions, acc, other_acc, twin_acc, twin_other, twin_sum, far, gathered,
+    local_sem, key_send, key_recv, val_send, val_recv, sum_send, sum_recv,
     up_send, down_send, cross_send, pair_send, line_recv, pair_recv,
 ):
     heads, size, _ = gate.shape
@@ -126,6 +126,16 @@
     core, chip = me % ROWS, me // ROWS
     y, z = chip % ROWS, chip // ROWS
     half = 3 * size // ROWS
+    near_lines = lines // 2
+    first_line = z // near_lines * near_lines
+
+    def opposite(line):
+        return (line + near_lines) % lines
+
+    def near(n):
+        return first_line + (z + n) % near_lines
+
+    twin = opposite(z) * ROWS + y
     piece = half // PIECES
 
     def device(a_chip, a_core):
@@ -150,6 +160,7 @@
         for i, (src, dst) in enumerate([
             (rates_hbm, rates_in), (values_hbm, values),
             (keys_hbm.at[:, columns(chip)], key_in.at[chip]),
+            (keys_hbm.at[:, columns(twin)], key_in.at[twin]),
             (queries_hbm, queries), (gate_hbm, gate), (up_hbm, up), (down_hbm, down),
             (questions_hbm, questions),
         ])
@@ -165,31 +176,38 @@
         weighted_out[head] = (
             rates[:, head:head + 1] * values[:, cols].astype(jnp.float32)
         ).astype(jnp.bfloat16)
-    own_weighted = pltpu.make_async_copy(weighted_out.at[chip], weighted_in.at[chip], local_sem.at[8])
+    own_weighted = [
+        pltpu.make_async_copy(weighted_out.at[head], weighted_in.at[head], local_sem.at[9 + i])
+        for i, head in enumerate((chip, twin))
+    ]
 
     pl.semaphore_wait(barrier, lines * ROWS)
-    own_weighted.start()
-
-    def key_copy(to, slot):
+    for load in own_weighted:
+        load.start()
+
+    def key_copy(head, to, slot):
         return pltpu.make_async_remote_copy(
-            src_ref=keys_hbm.at[:, columns(to)], dst_ref=key_in.at[slot],
-            send_sem=key_send.at[to], recv_sem=key_recv.at[slot],
+            src_ref=keys_hbm.at[:, columns(head)], dst_ref=key_in.at[slot],
+            send_sem=key_send.at[head], recv_sem=key_recv.at[slot],
             device_id=device(to, core), device_id_type=MESH)
 
-    def val_copy(to, slot):
+    def val_copy(head, to, slot):
         return pltpu.make_async_remote_copy(
-            src_ref=weighted_out.at[to], dst_ref=weighted_in.at[slot],
-            send_sem=val_send.at[to], recv_sem=val_recv.at[slot],
+            src_ref=weighted_out.at[head], dst_ref=weighted_in.at[slot],
+            send_sem=val_send.at[head], recv_sem=val_recv.at[slot],
             device_id=device(to, core), device_id_type=MESH)
 
-    for j in reversed(range(lines)):
-        for dy in range(ROWS):
-            if j or dy:
-                to = place(j) * ROWS + (y + dy) % ROWS
-                key_copy(to, chip).start()
-                val_copy(to, chip).start()
-
-    for load in loads[2:7]:
+    for side in (opposite, lambda line: line):
+        for n in reversed(range(near_lines)):
+            for dy in range(ROWS):
+                if n or dy:
+                    row = (y + dy) % ROWS
+                    head = side(near(n)) * ROWS + row
+                    slot = side(z) * ROWS + y
+                    key_copy(head, near(n) * ROWS + row, slot).start()
+                    val_copy(head, near(n) * ROWS + row, slot).start()
+
+    for load in loads[2:8]:
         load.wait()
 
     @pl.loop(0, heads)
@@ -197,26 +215,31 @@
         context_ref[:, columns(head)] = read_memory(
             queries[:, columns(head)], gate[head], up[head], down[head])
 
-    own_weighted.wait()
-    acc[...] = jnp.zeros_like(acc)
-
-    @pl.loop(0, lines)
-    def _(j):
-        line = place(j)
-        for a_row in range(ROWS):
-            source = line * ROWS + a_row
-
-            @pl.when(source != chip)
+    for load in own_weighted:
+        load.wait()
+
+    def gradients(head, side, sums):
+        sums[...] = jnp.zeros_like(sums)
+
+        @pl.loop(0, near_lines)
+        def _(n):
+            accumulate(near(n), head, side(near(n)), sums)
+
+    def accumulate(line, head, slots, sums):
+        for row in range(ROWS):
+            slot = slots * ROWS + row
+
+            @pl.when(line * ROWS + row != chip)
             def _():
-                key_copy(source, source).wait_recv()
-                val_copy(source, source).wait_recv()
-
-        pair = pl.ds(line * ROWS, ROWS)
+                key_copy(slot, chip, slot).wait_recv()
+                val_copy(slot, chip, slot).wait_recv()
+
+        pair = pl.ds(slots * ROWS, ROWS)
         key = key_in[pair].reshape(-1, size)
         weighted = weighted_in[pair].reshape(-1, size)
-        pre_gate = dot(key, gate[chip])
-        pre_up = dot(key, up[chip])
-        back_hidden = dot(weighted, down[chip], ((1,), (1,)))
+        pre_gate = dot(key, gate[head])
+        pre_up = dot(key, up[head])
+        back_hidden = dot(weighted, down[head], ((1,), (1,)))
         sigmoid = jax.nn.sigmoid(pre_gate)
         active = pre_gate * sigmoid
         hidden = (active * pre_up).astype(jnp.bfloat16)
@@ -224,19 +247,40 @@
             back_hidden * pre_up * sigmoid * (1.0 + pre_gate * (1.0 - sigmoid))
         ).astype(jnp.bfloat16)
         back_up = (back_hidden * active).astype(jnp.bfloat16)
-        acc[0] += dot(key, back_gate, ((0,), (0,)))
-        acc[1] += dot(key, back_up, ((0,), (0,)))
-        acc[2] += dot(hidden, weighted, ((0,), (0,)))
-
-    exchange = pltpu.make_async_remote_copy(
-        src_ref=acc, dst_ref=other_acc, send_sem=acc_send, recv_sem=acc_recv,
-        device_id=device(chip, 1 - core), device_id_type=MESH)
+        sums[0:size, :] += dot(key, back_gate, ((0,), (0,)))
+        sums[size:2 * size, :] += dot(key, back_up, ((0,), (0,)))
+        sums[2 * size:3 * size, :] += dot(hidden, weighted, ((0,), (0,)))
+
+    def send(i, src, dst, to_chip, to_core):
+        return pltpu.make_async_remote_copy(
+            src_ref=src, dst_ref=dst, send_sem=sum_send.at[i], recv_sem=sum_recv.at[i],
+            device_id=device(to_chip, to_core), device_id_type=MESH)
+
+    def part_of(a_core):
+        return pl.ds(pl.multiple_of(a_core * half, half), half)
+
+    gradients(twin, opposite, twin_acc)
+    fold = send(0, twin_acc.at[part_of(1 - core)], twin_other, chip, 1 - core)
+    fold.start()
+    fold.wait()
+    twin_sum[...] = (twin_acc[part_of(core), :] + twin_other[...]).astype(jnp.bfloat16)
+    across_half = send(1, twin_sum, far.at[part_of(core)], twin, core)
+    across_half.start()
+
+    gradients(chip, lambda line: line, acc)
+    exchange = send(2, acc, other_acc, chip, 1 - core)
     exchange.start()
     exchange.wait()
+    across_half.wait()
+    share = send(3, far.at[part_of(core)], far.at[part_of(core)], chip, 1 - core)
+    share.start()
+    share.wait_send()
+    send(3, far.at[part_of(1 - core)], far.at[part_of(1 - core)], chip, 1 - core).wait_recv()
 
     matrices = []
     for m in range(3):
-        total = acc[m] + other_acc[m]
+        rows = slice(m * size, (m + 1) * size)
+        total = (acc[rows, :] + other_acc[rows, :]) + far[rows, :].astype(jnp.float32)
         norm = jnp.sqrt(jnp.sum(total * total, keepdims=True))
         matrices.append((total / (norm + 1e-06)).astype(jnp.bfloat16))
     for _ in range(NS_STEPS):
@@ -314,7 +358,7 @@
             pl.when(has_down)(lambda: hop_down(across(z), p).start())
             hop_pair(across(z), p).start()
 
-    loads[7].wait()
+    loads[8].wait()
     answer(chip)
 
     def along(line, has_next, next_hop):
@@ -348,12 +392,12 @@
     def _(k):
         pl.when(z - k >= 0)(lambda: along(z - k, has_up, hop_up))
         pl.when(z + k < lines)(lambda: along(z + k, has_down, hop_down))
-        near = k - 1
+        step = k - 1
         last = k - 2
-        pl.when(z - near >= 0)(lambda: crossed(z - near))
-        pl.when((near > 0) & (z + near < lines))(lambda: crossed(z + near))
-        pl.when((near > 0) & (z - near >= 0))(lambda: finish(mine(z - near)))
-        pl.when((near > 0) & (z + near < lines))(lambda: finish(mine(z + near)))
+        pl.when(z - step >= 0)(lambda: crossed(z - step))
+        pl.when((step > 0) & (z + step < lines))(lambda: crossed(z + step))
+        pl.when((step > 0) & (z - step >= 0))(lambda: finish(mine(z - step)))
+        pl.when((step > 0) & (z + step < lines))(lambda: finish(mine(z + step)))
         pl.when((last >= 0) & (z - last >= 0))(lambda: finish(across(z - last)))
         pl.when((last > 0) & (z + last < lines))(lambda: finish(across(z + last)))
 
@@ -361,13 +405,13 @@
     def _(line):
         goes_up = (line <= z) & has_up
         goes_down = (line >= z) & has_down
-        key_copy(across(line), across(line)).wait_send()
-        val_copy(across(line), across(line)).wait_send()
-
-        @pl.when(line != z)
-        def _():
-            key_copy(mine(line), mine(line)).wait_send()
-            val_copy(mine(line), mine(line)).wait_send()
+        for row in range(ROWS):
+            head = line * ROWS + row
+
+            @pl.when((head != chip) & (head != twin))
+            def _():
+                key_copy(head, chip, head).wait_send()
+                val_copy(head, chip, head).wait_send()
 
         for p in range(PIECES):
             pl.when(goes_up & early(line))(lambda: hop_up(across(line), p).wait_send())
@@ -416,12 +460,14 @@
             pltpu.VMEM((heads, size, size), half_type),
             pltpu.VMEM((heads, size, size), half_type),
             pltpu.VMEM((capacity, width), half_type),
-            pltpu.VMEM((3, size, size), jnp.float32),
-            pltpu.VMEM((3, size, size), jnp.float32),
+            *[pltpu.VMEM((3 * size, size), jnp.float32)] * 3,
+            pltpu.VMEM((3 * size // ROWS, size), jnp.float32),
+            pltpu.VMEM((3 * size // ROWS, size), half_type),
+            pltpu.VMEM((3 * size, size), half_type),
             pltpu.VMEM((heads, 3 * size, size), half_type),
-            sem((9,)),
+            sem((11,)),
             sem((heads,)), sem((heads,)), sem((heads,)), sem((heads,)),
-            sem, sem,
+            sem((4,)), sem((4,)),
             *[sem((heads * PIECES,))] * 6,
         ],
         compiler_params=pltpu.CompilerParams(

time: 62.2 us -> 57 us (0.916)
  Pallas kernels: 58.8 us -> 53.6 us
    pallas_call x1, Pallas kernels: 58.8 us -> 53.6 us  [head_per_chip(): pl.pallas_call(functools.partial(memory_kernel, lines), out_shape=(jax.Sh...]
where the time goes in v3:
time: 57 us; the launch traced here: 56.8 us
  Pallas kernels  53.6 us (94%)
  between operations  1.29 us (2%)
  other arithmetic  1.12 us (2%)
  local copies, waits for them, and re-layouts  0.79 us (1%)
    pallas_call x1, Pallas kernels, head_per_chip(): pl.pallas_call(functools.partial(memory_kernel, lines), out_shape=(jax.Sh...  53.6 us

profile of v3, /device:TPU:0, one launch (start us, length us, event | category | flops | bytes accessed | tf_op | source)
XLA Modules:
  0.0 56.8 jit_solution(13666890305500099502)
XLA Ops:
  1.3 53.6 %shard_map.104 = (bf16[128,2048]{1,0:T(8,128)(2,1)S(1)}, bf16[256,2048]{1,0:T(8,128)(2,1)S(1)}) custom-call(bf16[128,2048]{1,0:T(8,128)(2,1)} %keys_hbm.1, bf16[128,2048]{1,0:T(8,128)(2,1)} %values_hbm.1, bf16[128,2048]{1,0:T(8,128)(2,1)} %queries_hbm.1, f32[8,128]{1,0:T(8,128)} %rates_hbm.1, bf16[8,256,256]{2,1,0:T(8,128)(2,1)} %gate_hbm.1, ...), custom_call_target="tpu_custom_call" | custom-call | tf_op jit(solution)/shard_map/pallas_call | solution.py:444
  54.9 1.1 %broadcast_select_fusion = bf16[256,2048]{1,0:T(8,128)(2,1)} fusion(bf16[256,2048]{1,0:T(8,128)(2,1)S(1)} %get-tuple-element.5, pred[256]{0:T(512)(128)(4,1)S(1)} %iota_compare_fusion), kind=kLoop, calls=%fused_computation | loop fusion | flops 524288 | bytes 2097408 | tf_op jit(solution)/shard_map/jit(_where)/select_n | solution.py:484
  56.0 0.8 %copy.13 = bf16[128,2048]{1,0:T(8,128)(2,1)} copy(bf16[128,2048]{1,0:T(8,128)(2,1)S(1)} %get-tuple-element.8) | data formatting | bytes 1048576
  (1 shorter events, 0.0 us)

commit v4 on v3

--- a/solution.py
+++ b/solution.py
@@ -256,26 +256,41 @@
             src_ref=src, dst_ref=dst, send_sem=sum_send.at[i], recv_sem=sum_recv.at[i],
             device_id=device(to_chip, to_core), device_id_type=MESH)
 
-    def part_of(a_core):
-        return pl.ds(pl.multiple_of(a_core * half, half), half)
+    third = half // 3
+
+    def part_of(a_core, p):
+        return pl.ds(pl.multiple_of(a_core * half + p * third, third), third)
 
     gradients(twin, opposite, twin_acc)
-    fold = send(0, twin_acc.at[part_of(1 - core)], twin_other, chip, 1 - core)
-    fold.start()
-    fold.wait()
-    twin_sum[...] = (twin_acc[part_of(core), :] + twin_other[...]).astype(jnp.bfloat16)
-    across_half = send(1, twin_sum, far.at[part_of(core)], twin, core)
-    across_half.start()
+    folds = [
+        send(p, twin_acc.at[part_of(1 - core, p)], twin_other.at[part_of(0, p)], chip, 1 - core)
+        for p in range(3)
+    ]
+    for fold in folds:
+        fold.start()
+    crossings = []
+    for p in range(3):
+        folds[p].wait_recv()
+        twin_sum[part_of(0, p), :] = (
+            twin_acc[part_of(core, p), :] + twin_other[part_of(0, p), :]
+        ).astype(jnp.bfloat16)
+        crossings.append(send(3 + p, twin_sum.at[part_of(0, p)], far.at[part_of(core, p)], twin, core))
+        crossings[p].start()
 
     gradients(chip, lambda line: line, acc)
-    exchange = send(2, acc, other_acc, chip, 1 - core)
+    exchange = send(9, acc, other_acc, chip, 1 - core)
     exchange.start()
     exchange.wait()
-    across_half.wait()
-    share = send(3, far.at[part_of(core)], far.at[part_of(core)], chip, 1 - core)
-    share.start()
-    share.wait_send()
-    send(3, far.at[part_of(1 - core)], far.at[part_of(1 - core)], chip, 1 - core).wait_recv()
+    shares = []
+    for p in range(3):
+        crossings[p].wait_recv()
+        shares.append(
+            send(6 + p, far.at[part_of(core, p)], far.at[part_of(core, p)], chip, 1 - core))
+        shares[p].start()
+    for p in range(3):
+        send(6 + p, far.at[part_of(1 - core, p)], far.at[part_of(1 - core, p)], chip, 1 - core).wait_recv()
+        for copy in (folds[p], crossings[p], shares[p]):
+            copy.wait_send()
 
     matrices = []
     for m in range(3):
@@ -467,7 +482,7 @@
             pltpu.VMEM((heads, 3 * size, size), half_type),
             sem((11,)),
             sem((heads,)), sem((heads,)), sem((heads,)), sem((heads,)),
-            sem((4,)), sem((4,)),
+            sem((10,)), sem((10,)),
             *[sem((heads * PIECES,))] * 6,
         ],
         compiler_params=pltpu.CompilerParams(

time: 57 us -> 55.6 us (0.975)
  Pallas kernels: 53.6 us -> 52.2 us
    pallas_call x1, Pallas kernels: 53.6 us -> 52.2 us  [head_per_chip(): pl.pallas_call(functools.partial(memory_kernel, lines), out_shape=(jax.Sh...]
where the time goes in v4:
time: 55.6 us; the launch traced here: 55.4 us
  Pallas kernels  52.2 us (94%)
  between operations  1.29 us (2%)
  other arithmetic  1.12 us (2%)
  local copies, waits for them, and re-layouts  0.79 us (1%)
    pallas_call x1, Pallas kernels, head_per_chip(): pl.pallas_call(functools.partial(memory_kernel, lines), out_shape=(jax.Sh...  52.2 us
    select_n x1, other arithmetic, head_per_chip(): jnp.where(live_mask[:, None], outputs, jnp.zeros_like(outputs))  1.11 us

profile of v4, /device:TPU:0, one launch (start us, length us, event | category | flops | bytes accessed | tf_op | source)
XLA Modules:
  0.0 55.4 jit_solution(17687016211396903569)
XLA Ops:
  1.3 52.2 %shard_map.104 = (bf16[128,2048]{1,0:T(8,128)(2,1)S(1)}, bf16[256,2048]{1,0:T(8,128)(2,1)S(1)}) custom-call(bf16[128,2048]{1,0:T(8,128)(2,1)} %keys_hbm.1, bf16[128,2048]{1,0:T(8,128)(2,1)} %values_hbm.1, bf16[128,2048]{1,0:T(8,128)(2,1)} %queries_hbm.1, f32[8,128]{1,0:T(8,128)} %rates_hbm.1, bf16[8,256,256]{2,1,0:T(8,128)(2,1)} %gate_hbm.1, ...), custom_call_target="tpu_custom_call" | custom-call | tf_op jit(solution)/shard_map/pallas_call | solution.py:459
  53.5 1.1 %broadcast_select_fusion = bf16[256,2048]{1,0:T(8,128)(2,1)} fusion(bf16[256,2048]{1,0:T(8,128)(2,1)S(1)} %get-tuple-element.5, pred[256]{0:T(512)(128)(4,1)S(1)} %iota_compare_fusion), kind=kLoop, calls=%fused_computation | loop fusion | flops 524288 | bytes 2097408 | tf_op jit(solution)/shard_map/jit(_where)/select_n | solution.py:499
  54.6 0.8 %copy.13 = bf16[128,2048]{1,0:T(8,128)(2,1)} copy(bf16[128,2048]{1,0:T(8,128)(2,1)S(1)} %get-tuple-element.8) | data formatting | bytes 1048576
  (1 shorter events, 0.0 us)
